TPU v7x, 512 devices: a whole 4x8x8 slice. The times are simulated.
512 devices in a mesh: freq: 4 (over z_hi), layer: 8 (over x, z_lo), lat: 16 (over y, core).
Axes of the slice: x: 4, y: 8, z: 8 (z_hi: 4, z_lo: 2; z = z_hi * 2 + z_lo), core: 2. Of those that a mesh axis runs over, the one named last changes fastest.
Arguments:
- source: float32 [2, 4, 2, 8, 512, 512], P(None, 'freq', None, 'layer', 'lat'), may hold values from -6 to 6
- contrast: float32 [2, 4, 8, 512, 512], P(None, 'freq', 'layer', 'lat'), may hold values from -0.5 to 0.5
- green: float32 [2, 4, 8, 8, 512, 512], P(None, 'freq', None, 'layer', 'lat'), may hold values from -0.6 to 0.6
- efield: float32 [2, 4, 2, 8, 512, 512], P(None, 'freq', None, 'layer', 'lat'), may hold values from -6 to 6
- cell_class: int32 [8, 512, 512], P('layer', 'lat'), may hold values from 0 to 7
Outputs:
- cell_gradient: float32 [8, 512, 512], P('layer', 'lat')
- class_gradient: float32 [8, 8], P('layer')
All inputs are finite; a program needn't handle non-finite values.
Results may differ from a plain program's by a relative error of at most 0.0001.
Values sent between devices are 32-bit elements; how exact they have to be, the bound alone decides.
A program may use at most 64 MiB of HBM per device.

v0:
```python
import math
import jax
import jax.numpy as jnp
from jax import lax
from jax.sharding import PartitionSpec as P

NXY = 512
ITERS = 2
CLASSES = 8
highest = lax.Precision.HIGHEST


def tables(length):
    index = jnp.arange(length, dtype=jnp.int32)
    phase = index[:, None] * index[None, :] % length
    angle = phase.astype(jnp.float32) * (2.0 * math.pi / length)
    factor = 1.0 / math.sqrt(length)
    return (jnp.cos(angle) * factor, jnp.sin(angle) * factor)


def forward(field, cosine, sine):
    first = jnp.einsum("zfplxy,yk->zfplkx", field, cosine, precision=highest)
    second = jnp.einsum("zfplxy,yk->zfplkx", field, sine, precision=highest)
    partial_spec = jnp.stack([first[0] + second[1], first[1] - second[0]])
    turned = lax.all_to_all(partial_spec, "lat", split_axis=4, concat_axis=5, tiled=True)
    first = jnp.einsum("zfplkx,xq->zfplkq", turned, cosine, precision=highest)
    second = jnp.einsum("zfplkx,xq->zfplkq", turned, sine, precision=highest)
    return jnp.stack([first[0] + second[1], first[1] - second[0]])


def inverse(mixed, cosine, sine):
    first = jnp.einsum("lzfpkq,qx->zfplkx", mixed, cosine, precision=highest)
    second = jnp.einsum("lzfpkq,qx->zfplkx", mixed, sine, precision=highest)
    half_back = jnp.stack([first[0] - second[1], first[1] + second[0]])
    turned = lax.all_to_all(half_back, "lat", split_axis=5, concat_axis=4, tiled=True)
    first = jnp.einsum("zfplkx,ky->zfplxy", turned, cosine, precision=highest)
    second = jnp.einsum("zfplkx,ky->zfplxy", turned, sine, precision=highest)
    return jnp.stack([first[0] - second[1], first[1] + second[0]])


def couple_product(left, right):
    return jnp.einsum("foiyx,fpiyx->ofpyx", left, right, precision=highest)


def couple(kernel, spectra):
    real_part = couple_product(kernel[0], spectra[0]) - couple_product(kernel[1], spectra[1])
    imag_part = couple_product(kernel[0], spectra[1]) + couple_product(kernel[1], spectra[0])
    return jnp.stack([real_part, imag_part], axis=1)


def cmul(factor, field):
    return jnp.stack(
        [factor[0] * field[0] - factor[1] * field[1], factor[0] * field[1] + factor[1] * field[0]]
    )


def per_device(source, contrast, green, efield, cell_class):
    cosine, sine = tables(source.shape[5])
    factor = contrast[:, :, None]
    field = source
    for step in range(ITERS):
        spectra = forward(cmul(factor, field), cosine, sine)
        mixed = lax.psum_scatter(couple(green, spectra), "layer", scatter_dimension=0, tiled=True)
        field = source + cmul(factor, inverse(mixed, cosine, sine))
    cell_terms = jnp.sum(efield[0] * field[0] - efield[1] * field[1], axis=(0, 1))
    cell = lax.psum(cell_terms, "freq")
    onehot = (cell_class[None] == jnp.arange(CLASSES, dtype=jnp.int32)[:, None, None, None]).astype(
        jnp.float32
    )
    local_sums = jnp.einsum("clxy,lxy->lc", onehot, cell, precision=highest) / float(NXY)
    classes = lax.psum(local_sums, "lat")
    return (cell, classes)


def solution(mesh):
    placed = (
        P(None, "freq", None, "layer", "lat", None),
        P(None, "freq", "layer", "lat", None),
        P(None, "freq", None, "layer", "lat", None),
        P(None, "freq", None, "layer", "lat", None),
        P("layer", "lat", None),
    )
    return jax.shard_map(
        per_device,
        mesh=mesh,
        in_specs=placed,
        out_specs=(P("layer", "lat", None), P("layer", None)),
        check_vma=False,
    )
```

profile of v0, /device:TPU:1, one launch (start us, length us, event | category | flops | bytes accessed | tf_op | source)
XLA Modules:
  0.0 504.2 jit_solution(15579151255789575674)
XLA Ops:
  9.1 4.9 convolution_bitcast_fusion.6
  14.0 4.9 convolution_bitcast_fusion.7
  19.7 1.7 reshape.508
  21.4 10.2 %all-to-all-start = ((f32[16,1,4096]{2,1,0:T(1,128)}), f32[16,1,4096]{2,1,0:T(1,128)S(1)}, u32[]{:S(2)}, u32[]{:S(2)}) async-start(f32[16,1,4096]{2,1,0:T(1,128)} %reshape.508), calls=%async_computation | async-start | bytes 524288 | tf_op jit(solution)/shard_map/all_to_all | solution.py:25
  31.9 11.4 %all-to-all-done = f32[16,1,4096]{2,1,0:T(1,128)S(1)} async-done(((f32[16,1,4096]{2,1,0:T(1,128)}), f32[16,1,4096]{2,1,0:T(1,128)S(1)}, u32[]{:S(2)}, u32[]{:S(2)}) %all-to-all-start) | async-done | bytes 262176 | tf_op jit(solution)/shard_map/all_to_all | solution.py:25
  47.1 4.9 fusion.14
  52.0 4.9 fusion.26
  57.2 1.5 pad_maximum_fusion
  59.0 1.3 dynamic-slice
  60.3 111.5 %all-reduce.8.cloned.1.call-done = f32[8,2,1,2,32,512]{5,4,3,0,2,1:T(8,128)} async-done(((f32[8,2,1,2,32,512]{5,4,3,0,2,1:T(8,128)}), f32[8,2,1,2,32,512]{5,4,3,0,2,1:T(8,128)}) %all-reduce.8.cloned.1.call-update) | async-done | bytes 2097168
  171.8 6.5 %convolution_bitcast_fusion.4 = f32[2,1,2,1,32,512]{5,4,2,0,1,3:T(8,128)S(1)} fusion(f32[8,2,1,2,32,512]{5,4,3,0,2,1:T(8,128)} %all-reduce.8.cloned.1.call-done, u32[]{:T(128)} %bitcast.104), kind=kOutput, calls=%fused_computation.9 | convolution fusion | flops 406585344 | bytes 524800 | tf_op jit(solution)/shard_map/lzfpkq,qx->zfplkx/dot_general | solution.py:33
  178.3 6.5 %convolution_bitcast_fusion.5 = f32[2,1,2,1,32,512]{5,4,2,0,1,3:T(8,128)S(1)} fusion(f32[8,2,1,2,32,512]{5,4,3,0,2,1:T(8,128)} %all-reduce.8.cloned.1.call-done, u32[]{:T(128)} %bitcast.104), kind=kOutput, calls=%fused_computation.10 | convolution fusion | flops 406585344 | bytes 524800 | tf_op jit(solution)/shard_map/lzfpkq,qx->zfplkx/dot_general | solution.py:32
  186.7 20.0 %all_to_all.60 = f32[16,1,4096]{2,1,0:T(1,128)S(1)} all-to-all(f32[16,1,4096]{2,1,0:T(1,128)S(1)} %reshape.510), channel_id=1, replica_groups=mesh['freq'=4,'layer'=8,'lat'=16] {'lat'}, dimensions={0} | all-to-all | bytes 524288 | tf_op jit(solution)/shard_map/all_to_all | solution.py:35
  206.7 1.3 reduce.3
  209.9 4.9 fusion.11
  214.8 4.9 fusion.23
  219.9 4.9 convolution_bitcast_fusion.3
  224.8 5.1 %convolution_bitcast_fusion.2 = f32[2,1,2,1,512,32]{4,5,2,0,3,1:T(8,128)S(1)} fusion(f32[1,1,2,1,32,512]{5,4,2,0,3,1:T(8,128)S(1)} %get-tuple-element.25, f32[1,1,2,1,32,512]{5,4,2,0,3,1:T(8,128)S(1)} %get-tuple-element.24), kind=kOutput, calls=%fused_computation.7 | convolution fusion | flops 406650880 | bytes 524288 | tf_op jit(solution)/shard_map/zfplxy,yk->zfplkx/dot_general | solution.py:23
  231.8 14.4 %all_to_all.61 = f32[16,1,4096]{2,1,0:T(1,128)S(1)} all-to-all(f32[16,1,4096]{2,1,0:T(1,128)S(1)} %reshape.512), channel_id=1, replica_groups=mesh['freq'=4,'layer'=8,'lat'=16] {'lat'}, dimensions={0} | all-to-all | bytes 524288 | tf_op jit(solution)/shard_map/all_to_all | solution.py:25
  249.4 4.9 fusion.20
  254.3 4.9 fusion.8
  259.6 1.5 pad_maximum_fusion.1
  261.1 109.4 %all-reduce.10.cloned.1.call-done = f32[8,2,1,2,32,512]{5,4,3,0,2,1:T(8,128)} async-done(((f32[8,2,1,2,32,512]{5,4,3,0,2,1:T(8,128)}), f32[8,2,1,2,32,512]{5,4,3,0,2,1:T(8,128)}) %all-reduce.10.cloned.1.call-update) | async-done | bytes 2097168
  370.6 6.7 %convolution_bitcast_fusion.1 = f32[2,1,2,1,32,512]{5,4,2,0,1,3:T(8,128)S(1)} fusion(f32[8,2,1,2,32,512]{5,4,3,0,2,1:T(8,128)} %all-reduce.10.cloned.1.call-done, u32[]{:T(128)} %bitcast.104), kind=kOutput, calls=%fused_computation.6 | convolution fusion | flops 406585344 | bytes 524800 | tf_op jit(solution)/shard_map/lzfpkq,qx->zfplkx/dot_general | solution.py:32
  377.3 6.5 %convolution_bitcast_fusion = f32[2,1,2,1,32,512]{5,4,2,0,1,3:T(8,128)S(1)} fusion(f32[8,2,1,2,32,512]{5,4,3,0,2,1:T(8,128)} %all-reduce.10.cloned.1.call-done, u32[]{:T(128)} %bitcast.104), kind=kOutput, calls=%fused_computation.5 | convolution fusion | flops 406585344 | bytes 524800 | tf_op jit(solution)/shard_map/lzfpkq,qx->zfplkx/dot_general | solution.py:33
  385.7 19.8 %all_to_all.62 = f32[16,1,4096]{2,1,0:T(1,128)S(1)} all-to-all(f32[16,1,4096]{2,1,0:T(1,128)S(1)} %reshape.514), channel_id=1, replica_groups=mesh['freq'=4,'layer'=8,'lat'=16] {'lat'}, dimensions={0} | all-to-all | bytes 524288 | tf_op jit(solution)/shard_map/all_to_all | solution.py:35
  408.8 4.9 fusion.17
  413.7 4.9 fusion.5
  419.5 48.6 %all-reduce.6.cloned.1.call-done = f32[1,32,512]{2,1,0:T(8,128)} async-done(((f32[1,32,512]{2,1,0:T(8,128)}), f32[1,32,512]{2,1,0:T(8,128)}) %all-reduce.6.cloned.1.call-update) | async-done | bytes 65552 | tf_op jit(solution)/shard_map/psum | solution.py:66
  468.2 1.6 fusion.1
  469.8 26.1 %psum.15 = f32[1,8]{1,0:T(1,128)} all-reduce(f32[1,8]{1,0:T(1,128)S(1)} %fusion.1), channel_id=1, replica_groups=mesh['freq'=4,'layer'=8,'lat'=16] {'lat'}, use_global_device_ids=true, to_apply=%region_4.5 | all-reduce | flops 8 | bytes 64 | tf_op jit(solution)/shard_map/psum | solution.py:71
  495.9 1.5 copy.70
  (59 shorter events, 22.4 us)
Async XLA Ops:
  18.9 12.9 %copy-start.1 = (f32[2,1,8,1,32,512]{5,4,3,2,1,0:T(8,128)S(1)}, f32[2,1,8,1,32,512]{5,4,3,2,1,0:T(8,128)}, u32[]{:S(2)}) copy-start(f32[2,1,8,1,32,512]{5,4,3,2,1,0:T(8,128)} %param.7) | copy-start | bytes 3145732
  21.4 21.9 %all-to-all-start = ((f32[16,1,4096]{2,1,0:T(1,128)}), f32[16,1,4096]{2,1,0:T(1,128)S(1)}, u32[]{:S(2)}, u32[]{:S(2)}) async-start(f32[16,1,4096]{2,1,0:T(1,128)} %reshape.508), calls=%async_computation | async-start | bytes 524288 | tf_op jit(solution)/shard_map/all_to_all | solution.py:25
  31.6 140.2 %all-reduce.8.cloned.1.call-start = ((), (), s32[]{:S(2)}) async-start(), calls=%async_computation.5 | async-start | bytes 4194304
  58.8 311.8 %all-reduce.10.cloned.1.call-start = ((), (), s32[]{:S(2)}) async-start(), calls=%async_computation.6 | async-start | bytes 4194304
  214.8 5.0 copy-start
  261.1 207.1 %all-reduce.6.cloned.1.call-start = ((), (), s32[]{:S(2)}) async-start(), calls=%async_computation.4 | async-start | bytes 131072 | tf_op jit(solution)/shard_map/psum | solution.py:66
  413.7 5.1 %copy-start.2 = (f32[2,1,2,1,32,512]{5,4,3,2,1,0:T(8,128)S(1)}, f32[2,1,2,1,32,512]{5,4,3,2,1,0:T(8,128)}, u32[]{:S(2)}) copy-start(f32[2,1,2,1,32,512]{5,4,3,2,1,0:T(8,128)} %param.8) | copy-start | bytes 786436
  418.6 0.8 copy-start.3
Sparse Core Ops, SparseCore 0:
  58.9 112.8 all-reduce.7
  261.2 109.3 all-reduce.9
  419.6 48.5 all-reduce.5
where the time goes:
time: 510 us; the launch traced here: 504 us
  waiting for transfers between devices  281 us (55%)
  matrix products  87.1 us (17%)
  blocking collectives  80.3 us (16%)
  local copies, waits for them, and re-layouts  19.7 us (4%)
  between operations  14.5 us (3%)
  other arithmetic  10.9 us (2%)
  starting transfers between devices  10.7 us (2%)
    unnamed x5, waiting for transfers between devices  221 us
    psum x1, waiting for transfers between devices, per_device(): cell = lax.psum(cell_terms, 'freq')  48.6 us
    all_to_all x2, blocking collectives, inverse(): lax.all_to_all(half_back, 'lat', split_axis=5, concat_axis=4, tiled=True)  39.8 us
    psum x1, blocking collectives, per_device(): classes = lax.psum(local_sums, 'lat')  26.1 us
    all_to_all x1, blocking collectives, forward(): lax.all_to_all(partial_spec, 'lat', split_axis=4, concat_axis=5, tiled=True)  14.4 us
    dot_general x2, matrix products, inverse(): first = jnp.einsum('lzfpkq,qx->zfplkx', mixed, cosine, precision=highest)  13.2 us
    dot_general x2, matrix products, inverse(): second = jnp.einsum('lzfpkq,qx->zfplkx', mixed, sine, precision=highest)  13.1 us
    all_to_all x1, waiting for transfers between devices, forward(): lax.all_to_all(partial_spec, 'lat', split_axis=4, concat_axis=5, tiled=True)  11.4 us
  transfers between devices with their start and end apart: 4, of which 4 were waited for; matrix products, arithmetic and copies ran while one was open for 0% of the time, Pallas kernels for 0%

commit v1 on v0

--- a/solution.py
+++ b/solution.py
@@ -63,7 +63,7 @@
         mixed = lax.psum_scatter(couple(green, spectra), "layer", scatter_dimension=0, tiled=True)
         field = source + cmul(factor, inverse(mixed, cosine, sine))
     cell_terms = jnp.sum(efield[0] * field[0] - efield[1] * field[1], axis=(0, 1))
-    cell = lax.psum(cell_terms, "freq")
+    cell = jnp.sum(lax.all_gather(cell_terms, "freq"), axis=0)
     onehot = (cell_class[None] == jnp.arange(CLASSES, dtype=jnp.int32)[:, None, None, None]).astype(
         jnp.float32
     )

time: 510 us -> 473 us (0.927)
  waiting for transfers between devices: 281 us -> 244 us
  starting transfers between devices: 10.7 us -> 18.8 us
  blocking collectives: 80.3 us -> 74 us
    psum x1 -> x0, waiting for transfers between devices: 48.6 us -> none  [per_device(): cell = lax.psum(cell_terms, 'freq')]
    all_to_all x2 -> x1, blocking collectives: 39.8 us -> 20 us  [inverse(): lax.all_to_all(half_back, 'lat', split_axis=5, concat_axis=4, tiled=True)]
    all_gather x0 -> x1, blocking collectives: none -> 14.5 us  [per_device(): cell = jnp.sum(lax.all_gather(cell_terms, 'freq'), axis=0)]
    all_to_all x0 -> x1, waiting for transfers between devices: none -> 11.5 us  [inverse(): lax.all_to_all(half_back, 'lat', split_axis=5, concat_axis=4, tiled=True)]
    all_to_all x0 -> x1, starting transfers between devices: none -> 8.22 us  [inverse(): lax.all_to_all(half_back, 'lat', split_axis=5, concat_axis=4, tiled=True)]
    unnamed x18 -> x19, local copies, waits for them, and re-layouts: 11.3 us -> 10.5 us
    unnamed x5 -> x4, waiting for transfers between devices: 221 us -> 221 us
where the time goes in v1:
time: 473 us; the launch traced here: 467 us
  waiting for transfers between devices  244 us (52%)
  matrix products  86.1 us (18%)
  blocking collectives  74 us (16%)
  local copies, waits for them, and re-layouts  18.9 us (4%)
  starting transfers between devices  18.8 us (4%)
  between operations  14.7 us (3%)
  other arithmetic  10.3 us (2%)
    unnamed x4, waiting for transfers between devices  221 us
    psum x1, blocking collectives, per_device(): classes = lax.psum(local_sums, 'lat')  25.1 us
    all_to_all x1, blocking collectives, inverse(): lax.all_to_all(half_back, 'lat', split_axis=5, concat_axis=4, tiled=True)  20 us
    all_to_all x1, blocking collectives, forward(): lax.all_to_all(partial_spec, 'lat', split_axis=4, concat_axis=5, tiled=True)  14.5 us
    all_gather x1, blocking collectives, per_device(): cell = jnp.sum(lax.all_gather(cell_terms, 'freq'), axis=0)  14.5 us
    dot_general x2, matrix products, inverse(): second = jnp.einsum('lzfpkq,qx->zfplkx', mixed, sine, precision=highest)  13.3 us
    dot_general x2, matrix products, inverse(): first = jnp.einsum('lzfpkq,qx->zfplkx', mixed, cosine, precision=highest)  13 us
    all_to_all x1, waiting for transfers between devices, inverse(): lax.all_to_all(half_back, 'lat', split_axis=5, concat_axis=4, tiled=True)  11.5 us
  transfers between devices with their start and end apart: 4, of which 4 were waited for; matrix products, arithmetic and copies ran while one was open for 0% of the time, Pallas kernels for 0%

profile of v1, /device:TPU:1, one launch (start us, length us, event | category | flops | bytes accessed | tf_op | source)
XLA Modules:
  0.0 466.9 jit_solution(5650668321114962912)
XLA Ops:
  9.1 4.9 %convolution_bitcast_fusion.6 = f32[2,1,2,1,512,32]{4,5,2,0,3,1:T(8,128)S(1)} fusion(f32[1,1,2,1,32,512]{5,4,2,0,3,1:T(8,128)S(1)} %get-tuple-element.27, f32[1,1,2,1,32,512]{5,4,2,0,3,1:T(8,128)S(1)} %get-tuple-element.26), kind=kOutput, calls=%fused_computation.11 | convolution fusion | flops 406650880 | bytes 524288 | tf_op jit(solution)/shard_map/zfplxy,yk->zfplkx/dot_general | solution.py:23
  14.0 4.9 %convolution_bitcast_fusion.7 = f32[2,1,2,1,512,32]{4,5,2,0,3,1:T(8,128)S(1)} fusion(f32[1,1,2,1,32,512]{5,4,2,0,3,1:T(8,128)S(1)} %get-tuple-element.27, f32[1,1,2,1,32,512]{5,4,2,0,3,1:T(8,128)S(1)} %get-tuple-element.26), kind=kOutput, calls=%fused_computation.12 | convolution fusion | flops 406650880 | bytes 524288 | tf_op jit(solution)/shard_map/zfplxy,yk->zfplkx/dot_general | solution.py:22
  19.7 1.7 reshape.510
  21.4 10.2 %all-to-all-start = ((f32[16,1,4096]{2,1,0:T(1,128)}), f32[16,1,4096]{2,1,0:T(1,128)S(1)}, u32[]{:S(2)}, u32[]{:S(2)}) async-start(f32[16,1,4096]{2,1,0:T(1,128)} %reshape.510), calls=%async_computation | async-start | bytes 524288 | tf_op jit(solution)/shard_map/all_to_all | solution.py:25
  31.9 11.4 %all-to-all-done = f32[16,1,4096]{2,1,0:T(1,128)S(1)} async-done(((f32[16,1,4096]{2,1,0:T(1,128)}), f32[16,1,4096]{2,1,0:T(1,128)S(1)}, u32[]{:S(2)}, u32[]{:S(2)}) %all-to-all-start) | async-done | bytes 262176 | tf_op jit(solution)/shard_map/all_to_all | solution.py:25
  47.1 4.9 %fusion.14 = f32[2,2,32,512]{3,2,1,0:T(8,128)S(1)} fusion(f32[2,2,32,512]{3,2,1,0:T(8,128)S(1)} %reshape.489), kind=kOutput, calls=%fused_computation.28 | convolution fusion | flops 406585344 | bytes 524288 | tf_op jit(solution)/shard_map/zfplkx,xq->zfplkq/dot_general | solution.py:27
  52.0 4.9 %fusion.26 = f32[2,2,32,512]{3,2,1,0:T(8,128)S(1)} fusion(f32[2,2,32,512]{3,2,1,0:T(8,128)S(1)} %reshape.489), kind=kOutput, calls=%fused_computation.40 | convolution fusion | flops 406585344 | bytes 524288 | tf_op jit(solution)/shard_map/zfplkx,xq->zfplkq/dot_general | solution.py:26
  57.3 1.5 pad_maximum_fusion
  59.0 1.3 dynamic-slice
  60.3 111.5 %all-reduce.5.cloned.1.call-done = f32[8,2,1,2,32,512]{5,4,3,0,2,1:T(8,128)} async-done(((f32[8,2,1,2,32,512]{5,4,3,0,2,1:T(8,128)}), f32[8,2,1,2,32,512]{5,4,3,0,2,1:T(8,128)}) %all-reduce.5.cloned.1.call-update) | async-done | bytes 2097168
  171.8 6.5 %convolution_bitcast_fusion.4 = f32[2,1,2,1,32,512]{5,4,2,0,1,3:T(8,128)S(1)} fusion(f32[8,2,1,2,32,512]{5,4,3,0,2,1:T(8,128)} %all-reduce.5.cloned.1.call-done, u32[]{:T(128)} %bitcast.104), kind=kOutput, calls=%fused_computation.9 | convolution fusion | flops 406585344 | bytes 524800 | tf_op jit(solution)/shard_map/lzfpkq,qx->zfplkx/dot_general | solution.py:33
  178.3 6.5 %convolution_bitcast_fusion.5 = f32[2,1,2,1,32,512]{5,4,2,0,1,3:T(8,128)S(1)} fusion(f32[8,2,1,2,32,512]{5,4,3,0,2,1:T(8,128)} %all-reduce.5.cloned.1.call-done, u32[]{:T(128)} %bitcast.104), kind=kOutput, calls=%fused_computation.10 | convolution fusion | flops 406585344 | bytes 524800 | tf_op jit(solution)/shard_map/lzfpkq,qx->zfplkx/dot_general | solution.py:32
  186.7 20.0 %all_to_all.60 = f32[16,1,4096]{2,1,0:T(1,128)S(1)} all-to-all(f32[16,1,4096]{2,1,0:T(1,128)S(1)} %reshape.512), channel_id=1, replica_groups=mesh['freq'=4,'layer'=8,'lat'=16] {'lat'}, dimensions={0} | all-to-all | bytes 524288 | tf_op jit(solution)/shard_map/all_to_all | solution.py:35
  206.7 1.3 reduce.5
  209.9 4.9 %fusion.11 = f32[2,2,32,512]{3,2,1,0:T(8,128)S(1)} fusion(f32[2,2,512,32]{2,3,1,0:T(8,128)S(1)} %reshape.493), kind=kOutput, calls=%fused_computation.25 | convolution fusion | flops 406585344 | bytes 524288 | tf_op jit(solution)/shard_map/zfplkx,ky->zfplxy/dot_general | solution.py:37
  214.8 4.9 %fusion.23 = f32[2,2,32,512]{3,2,1,0:T(8,128)S(1)} fusion(f32[2,2,512,32]{2,3,1,0:T(8,128)S(1)} %reshape.493), kind=kOutput, calls=%fused_computation.37 | convolution fusion | flops 406585344 | bytes 524288 | tf_op jit(solution)/shard_map/zfplkx,ky->zfplxy/dot_general | solution.py:36
  219.9 4.9 %convolution_bitcast_fusion.3 = f32[2,1,2,1,512,32]{4,5,2,0,3,1:T(8,128)S(1)} fusion(f32[1,1,2,1,32,512]{5,4,2,0,3,1:T(8,128)S(1)} %get-tuple-element.25, f32[1,1,2,1,32,512]{5,4,2,0,3,1:T(8,128)S(1)} %get-tuple-element.24), kind=kOutput, calls=%fused_computation.8 | convolution fusion | flops 406650880 | bytes 524288 | tf_op jit(solution)/shard_map/zfplxy,yk->zfplkx/dot_general | solution.py:22
  224.8 4.9 %convolution_bitcast_fusion.2 = f32[2,1,2,1,512,32]{4,5,2,0,3,1:T(8,128)S(1)} fusion(f32[1,1,2,1,32,512]{5,4,2,0,3,1:T(8,128)S(1)} %get-tuple-element.25, f32[1,1,2,1,32,512]{5,4,2,0,3,1:T(8,128)S(1)} %get-tuple-element.24), kind=kOutput, calls=%fused_computation.7 | convolution fusion | flops 406650880 | bytes 524288 | tf_op jit(solution)/shard_map/zfplxy,yk->zfplkx/dot_general | solution.py:23
  231.6 14.5 %all_to_all.61 = f32[16,1,4096]{2,1,0:T(1,128)S(1)} all-to-all(f32[16,1,4096]{2,1,0:T(1,128)S(1)} %reshape.514), channel_id=1, replica_groups=mesh['freq'=4,'layer'=8,'lat'=16] {'lat'}, dimensions={0} | all-to-all | bytes 524288 | tf_op jit(solution)/shard_map/all_to_all | solution.py:25
  249.3 4.9 %fusion.20 = f32[2,2,32,512]{3,2,1,0:T(8,128)S(1)} fusion(f32[2,2,32,512]{3,2,1,0:T(8,128)S(1)} %reshape.495), kind=kOutput, calls=%fused_computation.34 | convolution fusion | flops 406585344 | bytes 524288 | tf_op jit(solution)/shard_map/zfplkx,xq->zfplkq/dot_general | solution.py:26
  254.2 4.9 %fusion.8 = f32[2,2,32,512]{3,2,1,0:T(8,128)S(1)} fusion(f32[2,2,32,512]{3,2,1,0:T(8,128)S(1)} %reshape.495), kind=kOutput, calls=%fused_computation.22 | convolution fusion | flops 406585344 | bytes 524288 | tf_op jit(solution)/shard_map/zfplkx,xq->zfplkq/dot_general | solution.py:27
  259.5 1.5 pad_maximum_fusion.1
  261.1 109.5 %all-reduce.7.cloned.1.call-done = f32[8,2,1,2,32,512]{5,4,3,0,2,1:T(8,128)} async-done(((f32[8,2,1,2,32,512]{5,4,3,0,2,1:T(8,128)}), f32[8,2,1,2,32,512]{5,4,3,0,2,1:T(8,128)}) %all-reduce.7.cloned.1.call-update) | async-done | bytes 2097168
  370.6 6.5 %convolution_bitcast_fusion.1 = f32[2,1,2,1,32,512]{5,4,2,0,1,3:T(8,128)S(1)} fusion(f32[8,2,1,2,32,512]{5,4,3,0,2,1:T(8,128)} %all-reduce.7.cloned.1.call-done, u32[]{:T(128)} %bitcast.104), kind=kOutput, calls=%fused_computation.6 | convolution fusion | flops 406585344 | bytes 524800 | tf_op jit(solution)/shard_map/lzfpkq,qx->zfplkx/dot_general | solution.py:32
  377.1 6.8 %convolution_bitcast_fusion = f32[2,1,2,1,32,512]{5,4,2,0,1,3:T(8,128)S(1)} fusion(f32[8,2,1,2,32,512]{5,4,3,0,2,1:T(8,128)} %all-reduce.7.cloned.1.call-done, u32[]{:T(128)} %bitcast.104), kind=kOutput, calls=%fused_computation.5 | convolution fusion | flops 406585344 | bytes 524800 | tf_op jit(solution)/shard_map/lzfpkq,qx->zfplkx/dot_general | solution.py:33
  384.6 1.7 reshape.516
  386.4 8.2 %all-to-all-start.3 = ((f32[16,1,4096]{2,1,0:T(1,128)}), f32[16,1,4096]{2,1,0:T(1,128)S(1)}, u32[]{:S(2)}, u32[]{:S(2)}) async-start(f32[16,1,4096]{2,1,0:T(1,128)} %reshape.516), calls=%async_computation.3 | async-start | bytes 524288 | tf_op jit(solution)/shard_map/all_to_all | solution.py:35
  394.7 11.5 %all-to-all-done.3 = f32[16,1,4096]{2,1,0:T(1,128)S(1)} async-done(((f32[16,1,4096]{2,1,0:T(1,128)}), f32[16,1,4096]{2,1,0:T(1,128)S(1)}, u32[]{:S(2)}, u32[]{:S(2)}) %all-to-all-start.3) | async-done | bytes 262176 | tf_op jit(solution)/shard_map/all_to_all | solution.py:35
  409.4 4.9 %fusion.17 = f32[2,2,32,512]{3,2,1,0:T(8,128)S(1)} fusion(f32[2,2,512,32]{2,3,1,0:T(8,128)S(1)} %reshape.497), kind=kOutput, calls=%fused_computation.31 | convolution fusion | flops 406585344 | bytes 524288 | tf_op jit(solution)/shard_map/zfplkx,ky->zfplxy/dot_general | solution.py:36
  414.3 4.9 %fusion.5 = f32[2,2,32,512]{3,2,1,0:T(8,128)S(1)} fusion(f32[2,2,512,32]{2,3,1,0:T(8,128)S(1)} %reshape.497), kind=kOutput, calls=%fused_computation.19 | convolution fusion | flops 406585344 | bytes 524288 | tf_op jit(solution)/shard_map/zfplkx,ky->zfplxy/dot_general | solution.py:37
  419.4 14.5 %all-gather = f32[128,512]{1,0:T(8,128)S(1)} all-gather(f32[32,512]{1,0:T(8,128)S(1)} %fusion.34), channel_id=2, replica_groups=mesh['freq'=4,'layer'=8,'lat'=16] {'freq'}, dimensions={0}, use_global_device_ids=true | all-gather | bytes 327680 | tf_op jit(solution)/shard_map/all_gather | solution.py:66
  434.7 25.1 %psum.7 = f32[1,8]{1,0:T(1,128)} all-reduce(f32[1,8]{1,0:T(1,128)S(1)} %fusion.1), channel_id=1, replica_groups=mesh['freq'=4,'layer'=8,'lat'=16] {'lat'}, use_global_device_ids=true, to_apply=%region_4.5 | all-reduce | flops 8 | bytes 64 | tf_op jit(solution)/shard_map/psum | solution.py:71
  (60 shorter events, 21.5 us)
Async XLA Ops:
  18.9 12.9 %copy-start.1 = (f32[2,1,8,1,32,512]{5,4,3,2,1,0:T(8,128)S(1)}, f32[2,1,8,1,32,512]{5,4,3,2,1,0:T(8,128)}, u32[]{:S(2)}) copy-start(f32[2,1,8,1,32,512]{5,4,3,2,1,0:T(8,128)} %param.7) | copy-start | bytes 3145732
  21.4 21.9 %all-to-all-start = ((f32[16,1,4096]{2,1,0:T(1,128)}), f32[16,1,4096]{2,1,0:T(1,128)S(1)}, u32[]{:S(2)}, u32[]{:S(2)}) async-start(f32[16,1,4096]{2,1,0:T(1,128)} %reshape.510), calls=%async_computation | async-start | bytes 524288 | tf_op jit(solution)/shard_map/all_to_all | solution.py:25
  31.6 140.2 %all-reduce.5.cloned.1.call-start = ((), (), s32[]{:S(2)}) async-start(), calls=%async_computation.4 | async-start | bytes 4194304
  58.8 311.8 %all-reduce.7.cloned.1.call-start = ((), (), s32[]{:S(2)}) async-start(), calls=%async_computation.5 | async-start | bytes 4194304
  214.8 5.0 %copy-start = (f32[2,1,2,1,32,512]{5,4,3,2,1,0:T(8,128)S(1)}, f32[2,1,2,1,32,512]{5,4,3,2,1,0:T(8,128)}, u32[]{:S(2)}) copy-start(f32[2,1,2,1,32,512]{5,4,3,2,1,0:T(8,128)} %param.5) | copy-start | bytes 786436
  383.8 10.8 %copy-start.3 = (s32[1,32,512]{2,1,0:T(8,128)S(1)}, s32[1,32,512]{2,1,0:T(8,128)}, u32[]{:S(2)}) copy-start(s32[1,32,512]{2,1,0:T(8,128)} %param.9) | copy-start | bytes 196612
  386.4 19.8 %all-to-all-start.3 = ((f32[16,1,4096]{2,1,0:T(1,128)}), f32[16,1,4096]{2,1,0:T(1,128)S(1)}, u32[]{:S(2)}, u32[]{:S(2)}) async-start(f32[16,1,4096]{2,1,0:T(1,128)} %reshape.516), calls=%async_computation.3 | async-start | bytes 524288 | tf_op jit(solution)/shard_map/all_to_all | solution.py:35
  414.3 5.1 %copy-start.2 = (f32[2,1,2,1,32,512]{5,4,3,2,1,0:T(8,128)S(1)}, f32[2,1,2,1,32,512]{5,4,3,2,1,0:T(8,128)}, u32[]{:S(2)}) copy-start(f32[2,1,2,1,32,512]{5,4,3,2,1,0:T(8,128)} %param.8) | copy-start | bytes 786436
  433.9 25.9 %copy-start.4 = (f32[32,512]{1,0:T(8,128)}, f32[32,512]{1,0:T(8,128)S(1)}, u32[]{:S(2)}) copy-start(f32[32,512]{1,0:T(8,128)S(1)} %reduce.3) | copy-start | bytes 196612
Sparse Core Ops, SparseCore 0:
  58.9 112.8 all-reduce.4
  261.2 109.3 all-reduce.6
